TPU v7x, 128 devices: a whole 4x4x4 slice. The times are simulated.
128 devices in a mesh: dp: 8 (over z, core), fsdp: 16 (over x, y).
Axes of the slice: x: 4, y: 4, z: 4, core: 2. Of those that a mesh axis runs over, the one named last changes fastest.
Arguments:
- gate_act: bfloat16 [4096, 14848], P('fsdp', 'dp'), may hold values from -6 to 6
- up_act: bfloat16 [4096, 14848], P('fsdp', 'dp'), may hold values from -6 to 6
- out_grad: bfloat16 [4096, 4096], P('fsdp'), may hold values from -6 to 6
- master_old: float32 [8, 2176, 4096], P('dp', 'fsdp'), may hold values from -0.046875 to 0.046875
- moment1_old: float32 [8, 2176, 4096], P('dp', 'fsdp'), may hold values from -4 to 4
- moment2_old: float32 [8, 2176, 4096], P('dp', 'fsdp'), may hold values from 0.02 to 4
- old_bounds: int32 [8, 17], P('dp'), may hold values from 0 to 1856, as said below
- new_bounds: int32 [8, 16], P('dp'), may hold values from 0 to 1856, as said below
- rank_map: int32 [8, 16], P('dp'), may hold values from 0 to 15, as said below
Outputs:
- mlp_out: float32 [4096, 4096], P('fsdp', 'dp')
- master_new: float32 [8, 2176, 4096], P('dp', 'fsdp')
- moment1_new: float32 [8, 2176, 4096], P('dp', 'fsdp')
- moment2_new: float32 [8, 2176, 4096], P('dp', 'fsdp')
Inputs may be any that keep to these rules, and one draw needn't show every extreme that they name: Each row of old_bounds starts at 0, ends at 1856 and never falls; each position's rows fit its 136 slots. Each row of new_bounds starts at 0, ends at 1856 and never falls; each rank's rows fit 136 slots. In every block a position's new rows lie within its old rows and at most 58 rows of each of its two neighbours. `rank_map`: in each block's row exactly one position, one of the two middle ones, has rank 16 - 1 and owns nothing; the others hold the ranks 0 to 14 in position order.
All inputs are finite; a program needn't handle non-finite values.
Results may differ from a plain program's by a relative error of at most 0.012.
Values may be sent and summed in bfloat16 or wider, within the bound.
A program may use at most 192 MiB of HBM per device.

v0:
```python
import math

import jax
import jax.numpy as jnp
from jax import lax
from jax.sharding import PartitionSpec as P


def passed_along(value, axis, steps):
    count = lax.axis_size(axis)
    leading, last = (max(0, -steps), min(count, count - steps))
    return lax.ppermute(value, axis, [(source, source + steps) for source in range(leading, last)])


def pick_entry(table, index):
    return jnp.sum(jnp.where(jnp.arange(table.shape[0]) == index, table, jnp.zeros_like(table)))


def migrate(stacked, moved_rows, my_old_start, my_old_count, my_new_start, my_new_count):
    slot_rows = stacked.shape[1]
    prefix = stacked[:, :moved_rows]
    padded = jnp.concatenate(
        [jnp.zeros((3, moved_rows, stacked.shape[2]), stacked.dtype), stacked], axis=1
    )
    suffix = lax.dynamic_slice_in_dim(padded, my_old_count, moved_rows, 1)
    from_right = passed_along(prefix.astype(jnp.bfloat16), "fsdp", -1).astype(prefix.dtype)
    from_left = passed_along(suffix.astype(jnp.bfloat16), "fsdp", 1).astype(suffix.dtype)
    source = jnp.concatenate([from_left, stacked, from_right], axis=1)
    row_index = jnp.arange(slot_rows)
    global_row = my_new_start + row_index
    my_old_end = my_old_start + my_old_count
    index = (
        moved_rows
        + global_row
        - my_old_start
        + jnp.where(global_row >= my_old_end, slot_rows - my_old_count, 0)
    )
    index = jnp.clip(index, 0, 2 * moved_rows + slot_rows - 1)
    chosen = jnp.take(source, index, axis=1)
    return jnp.where((row_index < my_new_count)[None, :, None], chosen, jnp.zeros_like(chosen))


def block_product(hidden, weight_shard, table_start, table_count):
    slot_rows = weight_shard.shape[0]
    padded_hidden = jnp.concatenate(
        [hidden, jnp.zeros((hidden.shape[0], slot_rows), hidden.dtype)], axis=1
    )
    row_index = jnp.arange(slot_rows)[:, None]
    empty = jnp.zeros((hidden.shape[0], weight_shard.shape[1]), jnp.float32)
    piece = lax.all_gather(weight_shard, "fsdp", axis=0, tiled=True)
    shard_count = piece.shape[0] // slot_rows
    blocks = piece.reshape(shard_count, slot_rows, piece.shape[1])

    def one_shard(step, carry):
        start_col = pick_entry(table_start, step)
        live_rows = pick_entry(table_count, step)
        block = lax.dynamic_index_in_dim(blocks, step, 0, keepdims=False)
        block = jnp.where(row_index < live_rows, block, jnp.zeros_like(block))
        columns = lax.dynamic_slice_in_dim(padded_hidden, start_col, slot_rows, 1)
        return carry + jnp.dot(columns, block, preferred_element_type=jnp.float32)

    return lax.fori_loop(0, shard_count, one_shard, empty)


def local(
    gate_act,
    up_act,
    out_grad,
    master_old,
    moment1_old,
    moment2_old,
    old_bounds,
    new_bounds,
    rank_map,
):
    ranks_total = lax.axis_size("fsdp")
    my_position = lax.axis_index("fsdp")
    slot_rows = master_old.shape[1]
    token_rows = gate_act.shape[0]
    block_rows = gate_act.shape[1]
    base_rows = block_rows // ranks_total
    moved_rows = (base_rows + 1) // 2
    grad_scale = 1.0 / math.sqrt(token_rows * ranks_total)
    my_old_bounds = old_bounds[0]
    my_new_bounds = new_bounds[0]
    my_rank_map = rank_map[0]
    old_start = my_old_bounds[:-1]
    old_count = my_old_bounds[1:] - my_old_bounds[:-1]
    extended = jnp.concatenate([my_new_bounds, my_new_bounds[-1:]])
    extended_next = jnp.concatenate([extended[1:], extended[-1:]])
    owner_hit = my_rank_map[:, None] == jnp.arange(ranks_total + 1)[None, :]
    new_start = jnp.sum(jnp.where(owner_hit, extended[None, :], 0), axis=1)
    new_count = jnp.sum(jnp.where(owner_hit, extended_next[None, :], 0), axis=1) - new_start
    hidden = (jax.nn.silu(gate_act.astype(jnp.float32)) * up_act.astype(jnp.float32)).astype(
        jnp.bfloat16
    )
    stacked = jnp.stack([master_old[0], moment1_old[0], moment2_old[0]])
    moved = migrate(
        stacked,
        moved_rows,
        pick_entry(old_start, my_position),
        pick_entry(old_count, my_position),
        pick_entry(new_start, my_position),
        pick_entry(new_count, my_position),
    )
    weight_shard = moved[0].astype(jnp.bfloat16)
    block_part = block_product(hidden, weight_shard, new_start, new_count)
    mlp_out = lax.psum_scatter(
        block_part.astype(jnp.bfloat16), "dp", scatter_dimension=1, tiled=True
    ).astype(jnp.float32)
    row_index = jnp.arange(slot_rows * lax.axis_size("fsdp"))
    position = row_index // slot_rows
    within = row_index % slot_rows
    hit = position[:, None] == jnp.arange(ranks_total)[None, :]
    start_col = jnp.sum(jnp.where(hit, new_start[None, :], 0), axis=1)
    live_rows = jnp.sum(jnp.where(hit, new_count[None, :], 0), axis=1)
    column = jnp.clip(start_col + within, 0, block_rows - 1)
    chosen = jnp.take(hidden, column, axis=1)
    chosen = jnp.where((within < live_rows)[None, :], chosen, jnp.zeros_like(chosen))
    grad = (
        lax.psum_scatter(
            lax.dot_general(
                chosen, out_grad, (((0,), (0,)), ((), ())), preferred_element_type=jnp.float32
            ).astype(jnp.bfloat16),
            "fsdp",
            scatter_dimension=0,
            tiled=True,
        ).astype(jnp.float32)
        * grad_scale
    )
    first_next = 0.9 * moved[1] + 0.1 * grad
    second_next = 0.95 * moved[2] + 0.05 * grad * grad
    master_next = moved[0] - 0.001 * (first_next / (jnp.sqrt(second_next) + 1e-08) + 0.1 * moved[0])
    return (mlp_out, master_next[None], first_next[None], second_next[None])


def solution(mesh):
    placed = (
        P("fsdp", "dp"),
        P("fsdp", "dp"),
        P("fsdp", None),
        P("dp", "fsdp", None),
        P("dp", "fsdp", None),
        P("dp", "fsdp", None),
        P("dp", None),
        P("dp", None),
        P("dp", None),
    )
    return jax.shard_map(
        local,
        mesh=mesh,
        in_specs=placed,
        out_specs=(
            P("fsdp", "dp"),
            P("dp", "fsdp", None),
            P("dp", "fsdp", None),
            P("dp", "fsdp", None),
        ),
        check_vma=False,
    )
```

profile of v0, /device:TPU:0, one launch (start us, length us, event | category | flops | bytes accessed | tf_op | source)
XLA Modules:
  0.0 450.1 jit_solution(16102866951896543829)
XLA Ops:
  7.2 1.4 slice.37
  8.6 1.4 pad_add_fusion
  10.8 0.8 select_reduce_fusion.2
  11.6 1.5 fusion.42
  14.4 3.2 constant_dynamic-update-slice_fusion.2
  18.3 3.4 constant_dynamic-update-slice_fusion.1
  21.7 1.5 constant_dynamic-update-slice_fusion
  23.2 5.2 %fusion.10 = (bf16[3,58,4096]{2,1,0:T(8,128)(2,1)}, bf16[3,58,4096]{2,1,0:T(8,128)(2,1)}) fusion(s32[]{:T(128)S(6)} %select_n.170, f32[3,136,4096]{2,1,0:T(8,128)} %constant_dynamic-update-slice_fusion), kind=kLoop, calls=%fused_computation.23 | loop fusion | bytes 11108356 | tf_op jit(solution)/shard_map/convert_element_type | solution.py:27
  28.4 4.8 %collective-permute-start = (bf16[3,58,4096]{2,1,0:T(8,128)(2,1)}, bf16[3,58,4096]{2,1,0:T(8,128)(2,1)}, u32[]{:S(2)}, u32[]{:S(2)}) collective-permute-start(bf16[3,58,4096]{2,1,0:T(8,128)(2,1)} %get-tuple-element.207), channel_id=1, source_target_pairs={{0,1},{1,2},{2,3},{3,4},{4,5},{5,6},{6,7},{7,8},{8,9},{9,10},{10,1... | collective-permute-start | bytes 4276232 | tf_op jit(solution)/shard_map/ppermute | solution.py:12
  33.2 1.3 collective-permute-start.1
  37.1 1.2 compare_and_fusion.1
  38.4 1.2 compare_select_fusion.4
  39.6 26.3 %collective-permute-done = bf16[3,58,4096]{2,1,0:T(8,128)(2,1)} collective-permute-done((bf16[3,58,4096]{2,1,0:T(8,128)(2,1)}, bf16[3,58,4096]{2,1,0:T(8,128)(2,1)}, u32[]{:S(2)}, u32[]{:S(2)}) %collective-permute-start) | collective-permute-done | bytes 1425440 | tf_op jit(solution)/shard_map/ppermute | solution.py:12
  66.0 1.9 convert_element_type.38
  67.9 3.4 collective-permute-done.1
  71.3 1.7 convert_element_type.39
  73.1 2.1 pad_maximum_fusion
  75.1 23.1 %copy.39 = f32[3,252,4096]{2,0,1:T(4,128)} copy(f32[3,252,4096]{2,1,0:T(8,128)S(1)} %pad_maximum_fusion) | data formatting | bytes 24772608 | tf_op jit(solution)/shard_map/concatenate | solution.py:28
  98.2 17.2 %gather_fusion = f32[136,3,4096]{2,1,0:T(4,128)} fusion(f32[3,252,4096]{2,0,1:T(4,128)} %copy.39, s32[1024]{0:T(1024)S(1)} %pad_clamp_fusion.1), kind=kCustom, calls=%fused_computation | custom fusion | bytes 13369888 | tf_op jit(solution)/shard_map/jit(_take)/gather | solution.py:39
  115.4 12.2 %select_bitcast_fusion = f32[3,136,4096]{2,0,1:T(4,128)} fusion(f32[136,3,4096]{2,1,0:T(4,128)} %gather_fusion, pred[136]{0:T(512)(128)(4,1)S(1)} %iota_compare_fusion.2, pred[136]{0:T(512)(128)(4,1)S(1)} %compare_and_fusion.1), kind=kLoop, calls=%fused_computation.19 | loop fusion | flops 3342336 | bytes 13369616 | tf_op jit(solution)/shard_map/jit(_where)/select_n | solution.py:40
  127.7 16.3 %slice_multiply_fusion = (f32[1,136,4096]{2,0,1:T(1,128)}, f32[1,136,4096]{2,0,1:T(1,128)S(1)}, f32[1,136,4096]{2,0,1:T(1,128)}) fusion(f32[3,136,4096]{2,0,1:T(4,128)} %select_bitcast_fusion), kind=kLoop, calls=%fused_computation.30 | loop fusion | flops 557056 | bytes 13369344 | tf_op jit(solution)/shard_map/mul | solution.py:132
  144.0 1.4 copy-done.3
  145.3 2.2 copy.66
  147.8 2.1 fusion.20
  149.9 7.7 %gather_fusion.1 = bf16[2176,256]{1,0:T(8,128)(2,1)} fusion(bf16[256,1856]{0,1:T(8,128)(2,1)S(1)} %fusion.20, s32[3072]{0:T(1024)S(1)} %pad_clamp_fusion), kind=kCustom, calls=%fused_computation.1 | custom fusion | bytes 2236928 | tf_op jit(solution)/shard_map/jit(_take)/gather | solution.py:118
  157.6 10.2 %convolution_convert_fusion = bf16[2176,4096]{1,0:T(8,128)(2,1)} fusion(bf16[256,4096]{1,0:T(8,128)(2,1)S(1)} %copy-done, bf16[2176,256]{1,0:T(8,128)(2,1)} %gather_fusion.1, pred[2176]{0:T(1024)(128)(4,1)S(1)} %fusion.32, pred[2176]{0:T(1024)(128)(4,1)S(1)} %compare_and_fusion), kind=kOutput, calls=%fused_computation.16 | convolution fusion | flops 4573429760 | bytes 21041408 | tf_op jit(solution)/shard_map/dot_general | solution.py:122
  168.0 98.5 %all-gather.2.cloned.1.call-done = bf16[2176,4096]{1,0:T(8,128)(2,1)} async-done(((bf16[136,4096]{1,0:T(8,128)(2,1)}), bf16[2176,4096]{1,0:T(8,128)(2,1)}) %all-gather.2.cloned.1.call-update) | async-done | bytes 17825808 | tf_op jit(solution)/shard_map/all_gather | solution.py:50
  266.5 137.3 %while.14 = (s32[]{:T(128)}, f32[256,4096]{1,0:T(8,128)}, s32[16]{0:T(128)S(1)}, bf16[256,1992]{0,1:T(8,128)(2,1)S(1)}, s32[16]{0:T(128)S(1)}, /*index=5*/bf16[1...) while((s32[]{:T(128)}, f32[256,4096]{1,0:T(8,128)}, s32[16]{0:T(128)S(1)}, ...), condition=%wide.region_9.10_spmd.clone, body=%wide.region_6.9_spmd.clone.sunk | while | flops 287867104 | bytes 9573797 | solution.py:62
  269.7 4.0 convolution_add_fusion.2
  277.0 5.8 %convolution_add_fusion.2 = f32[256,4096]{1,0:T(8,128)} fusion(f32[256,4096]{1,0:T(8,128)} %get-tuple-element.267, pred[]{:T(512)S(6)} %compare.5, bf16[16,136,4096]{2,1,0:T(8,128)(2,1)} %get-tuple-element.280, s32[]{:T(128)} %get-tuple-element.266, pred[136]{0:T(512)(128)(4,1)S(1)} %compare_reduce_fusion.2, ...), kind=kOutput, calls=%fused_computation.3.clone.1 | convolution fusion | flops 287866880 | bytes 9573381 | tf_op jit(solution)/shard_map/while/body/eval_jaxpr/dot_general | solution.py:60
  286.1 5.4 %convolution_add_fusion.2 = f32[256,4096]{1,0:T(8,128)} fusion(f32[256,4096]{1,0:T(8,128)} %get-tuple-element.267, pred[]{:T(512)S(6)} %compare.5, bf16[16,136,4096]{2,1,0:T(8,128)(2,1)} %get-tuple-element.280, s32[]{:T(128)} %get-tuple-element.266, pred[136]{0:T(512)(128)(4,1)S(1)} %compare_reduce_fusion.2, ...), kind=kOutput, calls=%fused_computation.3.clone.1 | convolution fusion | flops 287866880 | bytes 9573381 | tf_op jit(solution)/shard_map/while/body/eval_jaxpr/dot_general | solution.py:60
  294.7 5.3 %convolution_add_fusion.2 = f32[256,4096]{1,0:T(8,128)} fusion(f32[256,4096]{1,0:T(8,128)} %get-tuple-element.267, pred[]{:T(512)S(6)} %compare.5, bf16[16,136,4096]{2,1,0:T(8,128)(2,1)} %get-tuple-element.280, s32[]{:T(128)} %get-tuple-element.266, pred[136]{0:T(512)(128)(4,1)S(1)} %compare_reduce_fusion.2, ...), kind=kOutput, calls=%fused_computation.3.clone.1 | convolution fusion | flops 287866880 | bytes 9573381 | tf_op jit(solution)/shard_map/while/body/eval_jaxpr/dot_general | solution.py:60
  303.3 5.5 %convolution_add_fusion.2 = f32[256,4096]{1,0:T(8,128)} fusion(f32[256,4096]{1,0:T(8,128)} %get-tuple-element.267, pred[]{:T(512)S(6)} %compare.5, bf16[16,136,4096]{2,1,0:T(8,128)(2,1)} %get-tuple-element.280, s32[]{:T(128)} %get-tuple-element.266, pred[136]{0:T(512)(128)(4,1)S(1)} %compare_reduce_fusion.2, ...), kind=kOutput, calls=%fused_computation.3.clone.1 | convolution fusion | flops 287866880 | bytes 9573381 | tf_op jit(solution)/shard_map/while/body/eval_jaxpr/dot_general | solution.py:60
  312.1 5.4 %convolution_add_fusion.2 = f32[256,4096]{1,0:T(8,128)} fusion(f32[256,4096]{1,0:T(8,128)} %get-tuple-element.267, pred[]{:T(512)S(6)} %compare.5, bf16[16,136,4096]{2,1,0:T(8,128)(2,1)} %get-tuple-element.280, s32[]{:T(128)} %get-tuple-element.266, pred[136]{0:T(512)(128)(4,1)S(1)} %compare_reduce_fusion.2, ...), kind=kOutput, calls=%fused_computation.3.clone.1 | convolution fusion | flops 287866880 | bytes 9573381 | tf_op jit(solution)/shard_map/while/body/eval_jaxpr/dot_general | solution.py:60
  320.7 5.4 %convolution_add_fusion.2 = f32[256,4096]{1,0:T(8,128)} fusion(f32[256,4096]{1,0:T(8,128)} %get-tuple-element.267, pred[]{:T(512)S(6)} %compare.5, bf16[16,136,4096]{2,1,0:T(8,128)(2,1)} %get-tuple-element.280, s32[]{:T(128)} %get-tuple-element.266, pred[136]{0:T(512)(128)(4,1)S(1)} %compare_reduce_fusion.2, ...), kind=kOutput, calls=%fused_computation.3.clone.1 | convolution fusion | flops 287866880 | bytes 9573381 | tf_op jit(solution)/shard_map/while/body/eval_jaxpr/dot_general | solution.py:60
  329.4 5.4 %convolution_add_fusion.2 = f32[256,4096]{1,0:T(8,128)} fusion(f32[256,4096]{1,0:T(8,128)} %get-tuple-element.267, pred[]{:T(512)S(6)} %compare.5, bf16[16,136,4096]{2,1,0:T(8,128)(2,1)} %get-tuple-element.280, s32[]{:T(128)} %get-tuple-element.266, pred[136]{0:T(512)(128)(4,1)S(1)} %compare_reduce_fusion.2, ...), kind=kOutput, calls=%fused_computation.3.clone.1 | convolution fusion | flops 287866880 | bytes 9573381 | tf_op jit(solution)/shard_map/while/body/eval_jaxpr/dot_general | solution.py:60
  338.1 5.4 %convolution_add_fusion.2 = f32[256,4096]{1,0:T(8,128)} fusion(f32[256,4096]{1,0:T(8,128)} %get-tuple-element.267, pred[]{:T(512)S(6)} %compare.5, bf16[16,136,4096]{2,1,0:T(8,128)(2,1)} %get-tuple-element.280, s32[]{:T(128)} %get-tuple-element.266, pred[136]{0:T(512)(128)(4,1)S(1)} %compare_reduce_fusion.2, ...), kind=kOutput, calls=%fused_computation.3.clone.1 | convolution fusion | flops 287866880 | bytes 9573381 | tf_op jit(solution)/shard_map/while/body/eval_jaxpr/dot_general | solution.py:60
  346.7 5.4 %convolution_add_fusion.2 = f32[256,4096]{1,0:T(8,128)} fusion(f32[256,4096]{1,0:T(8,128)} %get-tuple-element.267, pred[]{:T(512)S(6)} %compare.5, bf16[16,136,4096]{2,1,0:T(8,128)(2,1)} %get-tuple-element.280, s32[]{:T(128)} %get-tuple-element.266, pred[136]{0:T(512)(128)(4,1)S(1)} %compare_reduce_fusion.2, ...), kind=kOutput, calls=%fused_computation.3.clone.1 | convolution fusion | flops 287866880 | bytes 9573381 | tf_op jit(solution)/shard_map/while/body/eval_jaxpr/dot_general | solution.py:60
  355.4 5.3 %convolution_add_fusion.2 = f32[256,4096]{1,0:T(8,128)} fusion(f32[256,4096]{1,0:T(8,128)} %get-tuple-element.267, pred[]{:T(512)S(6)} %compare.5, bf16[16,136,4096]{2,1,0:T(8,128)(2,1)} %get-tuple-element.280, s32[]{:T(128)} %get-tuple-element.266, pred[136]{0:T(512)(128)(4,1)S(1)} %compare_reduce_fusion.2, ...), kind=kOutput, calls=%fused_computation.3.clone.1 | convolution fusion | flops 287866880 | bytes 9573381 | tf_op jit(solution)/shard_map/while/body/eval_jaxpr/dot_general | solution.py:60
  364.0 5.3 %convolution_add_fusion.2 = f32[256,4096]{1,0:T(8,128)} fusion(f32[256,4096]{1,0:T(8,128)} %get-tuple-element.267, pred[]{:T(512)S(6)} %compare.5, bf16[16,136,4096]{2,1,0:T(8,128)(2,1)} %get-tuple-element.280, s32[]{:T(128)} %get-tuple-element.266, pred[136]{0:T(512)(128)(4,1)S(1)} %compare_reduce_fusion.2, ...), kind=kOutput, calls=%fused_computation.3.clone.1 | convolution fusion | flops 287866880 | bytes 9573381 | tf_op jit(solution)/shard_map/while/body/eval_jaxpr/dot_general | solution.py:60
  372.6 5.4 %convolution_add_fusion.2 = f32[256,4096]{1,0:T(8,128)} fusion(f32[256,4096]{1,0:T(8,128)} %get-tuple-element.267, pred[]{:T(512)S(6)} %compare.5, bf16[16,136,4096]{2,1,0:T(8,128)(2,1)} %get-tuple-element.280, s32[]{:T(128)} %get-tuple-element.266, pred[136]{0:T(512)(128)(4,1)S(1)} %compare_reduce_fusion.2, ...), kind=kOutput, calls=%fused_computation.3.clone.1 | convolution fusion | flops 287866880 | bytes 9573381 | tf_op jit(solution)/shard_map/while/body/eval_jaxpr/dot_general | solution.py:60
  381.2 5.4 %convolution_add_fusion.2 = f32[256,4096]{1,0:T(8,128)} fusion(f32[256,4096]{1,0:T(8,128)} %get-tuple-element.267, pred[]{:T(512)S(6)} %compare.5, bf16[16,136,4096]{2,1,0:T(8,128)(2,1)} %get-tuple-element.280, s32[]{:T(128)} %get-tuple-element.266, pred[136]{0:T(512)(128)(4,1)S(1)} %compare_reduce_fusion.2, ...), kind=kOutput, calls=%fused_computation.3.clone.1 | convolution fusion | flops 287866880 | bytes 9573381 | tf_op jit(solution)/shard_map/while/body/eval_jaxpr/dot_general | solution.py:60
  389.9 5.3 %convolution_add_fusion.2 = f32[256,4096]{1,0:T(8,128)} fusion(f32[256,4096]{1,0:T(8,128)} %get-tuple-element.267, pred[]{:T(512)S(6)} %compare.5, bf16[16,136,4096]{2,1,0:T(8,128)(2,1)} %get-tuple-element.280, s32[]{:T(128)} %get-tuple-element.266, pred[136]{0:T(512)(128)(4,1)S(1)} %compare_reduce_fusion.2, ...), kind=kOutput, calls=%fused_computation.3.clone.1 | convolution fusion | flops 287866880 | bytes 9573381 | tf_op jit(solution)/shard_map/while/body/eval_jaxpr/dot_general | solution.py:60
  398.5 5.3 %convolution_add_fusion.2 = f32[256,4096]{1,0:T(8,128)} fusion(f32[256,4096]{1,0:T(8,128)} %get-tuple-element.267, pred[]{:T(512)S(6)} %compare.5, bf16[16,136,4096]{2,1,0:T(8,128)(2,1)} %get-tuple-element.280, s32[]{:T(128)} %get-tuple-element.266, pred[136]{0:T(512)(128)(4,1)S(1)} %compare_reduce_fusion.2, ...), kind=kOutput, calls=%fused_computation.3.clone.1 | convolution fusion | flops 287866880 | bytes 9573381 | tf_op jit(solution)/shard_map/while/body/eval_jaxpr/dot_general | solution.py:60
  403.8 3.8 convert_element_type.41
  407.7 12.8 %fusion.24 = (f32[1,136,4096]{2,1,0:T(8,128)}, f32[1,136,4096]{2,1,0:T(8,128)}, f32[1,136,4096]{2,1,0:T(8,128)}) fusion(bf16[136,4096]{1,0:T(8,128)(2,1)} %reduce-scatter.7.cloned.1.call-done, f32[1,136,4096]{2,0,1:T(1,128)} %get-tuple-element.204, f32[1,136,4096]{2,0,1:T(1,128)} %get-tuple-element.206, f32[1,136,4096]{2,0,1:T(1,128)} %copy-done.3), kind=kLoop, calls=%fused_computation.44 | loop fusion | flops 7798784 | bytes 14483456 | tf_op jit(solution)/shard_map/broadcast_in_dim | solution.py:134
  420.5 21.3 %reduce-scatter.5.cloned.1.call-done = bf16[256,512]{1,0:T(8,128)(2,1)} async-done(((bf16[256,4096]{1,0:T(8,128)(2,1)}), bf16[256,512]{1,0:T(8,128)(2,1)}) %reduce-scatter.5.cloned.1.call-update) | async-done | bytes 262160 | tf_op jit(solution)/shard_map/reduce_scatter | solution.py:108
  441.8 1.8 convert_element_type.42
  (60 shorter events, 22.9 us)
Async XLA Ops:
  7.2 150.4 %copy-start = (bf16[256,4096]{1,0:T(8,128)(2,1)S(1)}, bf16[256,4096]{1,0:T(8,128)(2,1)}, u32[]{:S(2)}) copy-start(bf16[256,4096]{1,0:T(8,128)(2,1)} %param.13) | copy-start | bytes 6291460
  7.2 259.3 %all-gather.2.cloned.1.call-start = ((), (), s32[]{:S(2)}) async-start(), calls=%async_computation.2 | async-start | bytes 18939904 | tf_op jit(solution)/shard_map/all_gather | solution.py:50
  18.3 3.4 copy-start.4
  28.4 37.5 %collective-permute-start = (bf16[3,58,4096]{2,1,0:T(8,128)(2,1)}, bf16[3,58,4096]{2,1,0:T(8,128)(2,1)}, u32[]{:S(2)}, u32[]{:S(2)}) collective-permute-start(bf16[3,58,4096]{2,1,0:T(8,128)(2,1)} %get-tuple-element.207), channel_id=1, source_target_pairs={{0,1},{1,2},{2,3},{3,4},{4,5},{5,6},{6,7},{7,8},{8,9},{9,10},{10,1... | collective-permute-start | bytes 4276232 | tf_op jit(solution)/shard_map/ppermute | solution.py:12
  33.2 38.1 %collective-permute-start.1 = (bf16[3,58,4096]{2,1,0:T(8,128)(2,1)}, bf16[3,58,4096]{2,1,0:T(8,128)(2,1)}, u32[]{:S(2)}, u32[]{:S(2)}) collective-permute-start(bf16[3,58,4096]{2,1,0:T(8,128)(2,1)} %get-tuple-element.208), channel_id=1, source_target_pairs={{1,0},{2,1},{3,2},{4,3},{5,4},{6,5},{7,6},{8,7},{9,8},{10,9},{11,1... | collective-permute-start | bytes 4276232 | tf_op jit(solution)/shard_map/ppermute | solution.py:12
  65.9 7.1 %copy-start.2 = (f32[3,136,4096]{2,1,0:T(8,128)S(1)}, f32[3,136,4096]{2,1,0:T(8,128)}, u32[]{:S(2)}) copy-start(f32[3,136,4096]{2,1,0:T(8,128)} %constant_dynamic-update-slice_fusion) | copy-start | bytes 20054020
  143.9 1.4 copy-start.3
  147.5 260.1 %reduce-scatter.7.cloned.1.call-start = ((), (), s32[]{:S(2)}) async-start(), calls=%async_computation.4 | async-start | bytes 18939904
  167.9 273.9 %reduce-scatter.5.cloned.1.call-start = ((), (), s32[]{:S(2)}) async-start(), calls=%async_computation.3 | async-start | bytes 2359296 | tf_op jit(solution)/shard_map/reduce_scatter | solution.py:108
  407.6 35.9 %copy-start.1 = (bf16[256,4096]{1,0:T(8,128)(2,1)S(1)}, bf16[256,4096]{1,0:T(8,128)(2,1)}, u32[]{:S(2)}) copy-start(bf16[256,4096]{1,0:T(8,128)(2,1)} %param.13) | copy-start | bytes 6291460
Sparse Core Ops, SparseCore 0:
  147.6 118.7 all-gather.1
  269.9 115.5 reduce-scatter.6
  407.7 34.0 reduce-scatter.4
where the time goes:
time: 451 us; the launch traced here: 450 us
  waiting for transfers between devices  150 us (33%)
  matrix products  95.4 us (21%)
  other arithmetic  83.4 us (18%)
  local copies, waits for them, and re-layouts  66.4 us (15%)
  loops' own time  31.3 us (7%)
  between operations  17.8 us (4%)
  starting transfers between devices  6.23 us (1%)
    all_gather x1, waiting for transfers between devices, block_product(): piece = lax.all_gather(weight_shard, 'fsdp', axis=0, tiled=True)  98.5 us
    dot_general x16, matrix products, one_shard(): return carry + jnp.dot(columns, block, preferred_element_type=jnp.float32)  85.1 us
    another operation x1, loops' own time, block_product(): return lax.fori_loop(0, shard_count, one_shard, empty)  31.3 us
    ppermute x2, waiting for transfers between devices, passed_along(): lax.ppermute(value, axis, [(source, source + steps) for source in range(l...  29.8 us
    concatenate x1, local copies, waits for them, and re-layouts, migrate(): source = jnp.concatenate([from_left, stacked, from_right], axis=1)  23.1 us
    reduce_scatter x1, waiting for transfers between devices, local(): lax.psum_scatter(block_part.astype(jnp.bfloat16), 'dp', scatter_dimension...  21.3 us
    gather x1, local copies, waits for them, and re-layouts, migrate(): chosen = jnp.take(source, index, axis=1)  17.2 us
    mul x1, other arithmetic, local(): second_next = 0.95 * moved[2] + 0.05 * grad * grad  16.3 us
  transfers between devices with their start and end apart: 5, of which 4 were waited for; matrix products, arithmetic and copies ran while one was open for 33% of the time, Pallas kernels for 0%

commit v1 on v0

v1 whole, which is shorter than its diff:
```python
import functools
import math

import jax
import jax.numpy as jnp
from jax import lax
from jax.experimental import pallas as pl
from jax.experimental.pallas import tpu as pltpu
from jax.sharding import PartitionSpec as P

BF = jnp.bfloat16
F32 = jnp.float32
MESH = pl.DeviceIdType.MESH

SIDE = 4
POS = 16
CAP = 136
PITCH = 144
HID = 1856
HIDP = 1920
D = 4096
COLS = D // SIDE
TOK = 256
EDGE = 64
SLACK = 320
HALF = 2 * PITCH
SLOTS = POS * PITCH
OFFS = (0, 1, 3, 2)


def window(first, size):
    low, high = HIDP, 0
    for p in range(POS):
        r0 = max(0, first - p * PITCH)
        r1 = min(CAP, first + size - p * PITCH)
        if r0 < r1:
            low = min(low, max(0, CAP * p - SLACK) + r0)
            high = max(high, min(HID, CAP * p) + r1)
    high = min(high, HID)
    low = low // 128 * 128
    high = -(-high // 128) * 128
    return low, high - low


NEW_WIN = [window(HALF * b, HALF) for b in range(8)]
OLD_WIN = [window(256 * b, 256) for b in range(SLOTS // 256)]
NEW_MAX = max(w for _, w in NEW_WIN)
OLD_MAX = max(w for _, w in OLD_WIN)


def prep_kernel(ob, nb, rm, gate, up, master, first, second, tab, hid, wq, pre, suf, buf):
    step = pl.program_id(0)
    me = lax.axis_index("fsdp")

    @pl.when(step == 0)
    def _():
        for p in range(POS):
            tab[0, p] = ob[0, p]
            tab[1, p] = ob[0, p + 1] - ob[0, p]
            k = rm[0, p]
            start = nb[0, k]
            tab[2, p] = start
            tab[3, p] = nb[0, jnp.minimum(k + 1, POS - 1)] - start
        buf[:, pl.ds(0, EDGE), :] = jnp.zeros((buf.shape[0], EDGE, 128), F32)

    g = gate[...].astype(F32)
    h = (g * jax.nn.sigmoid(g) * up[...].astype(F32)).astype(BF)
    hid[:, pl.ds(0, HID)] = h
    hid[:, pl.ds(HID, HIDP - HID)] = jnp.zeros((h.shape[0], HIDP - HID), BF)

    count = ob[0, me + 1] - ob[0, me]
    wq[0, pl.ds(0, CAP), :] = master[0].astype(BF)
    wq[0, pl.ds(CAP, PITCH - CAP), :] = jnp.zeros((PITCH - CAP, COLS), BF)
    for a, ref in enumerate((master, first, second)):
        pre[a] = ref[0, pl.ds(0, EDGE), :].astype(BF)
        for j in range(COLS // 128):
            lanes = pl.ds(128 * j, 128)
            buf[j, pl.ds(EDGE, CAP), :] = ref[0, :, lanes]
            suf[a, :, lanes] = buf[j, pl.ds(count, EDGE), :].astype(BF)


def prep(ob, nb, rm, gate, up, master, first, second):
    state = pl.BlockSpec((1, CAP, COLS), lambda i: (0, 0, i))
    act = pl.BlockSpec((TOK // 4, HID), lambda i: (i, 0))
    smem = pl.BlockSpec(memory_space=pltpu.SMEM)
    edge = pl.BlockSpec((3, EDGE, COLS), lambda i: (0, 0, i))
    return pl.pallas_call(
        prep_kernel,
        grid=(4,),
        in_specs=[smem, smem, smem, act, act, state, state, state],
        out_specs=[
            smem,
            pl.BlockSpec((TOK // 4, HIDP), lambda i: (i, 0)),
            pl.BlockSpec((1, PITCH, COLS), lambda i: (i, 0, 0)),
            edge,
            edge,
        ],
        out_shape=[
            jax.ShapeDtypeStruct((4, POS), jnp.int32),
            jax.ShapeDtypeStruct((TOK, HIDP), BF),
            jax.ShapeDtypeStruct((SIDE, PITCH, COLS), BF),
            jax.ShapeDtypeStruct((3, EDGE, D), BF),
            jax.ShapeDtypeStruct((3, EDGE, D), BF),
        ],
        scratch_shapes=[pltpu.VMEM((COLS // 128, EDGE + CAP + EDGE, 128), F32)],
        name="prep",
    )(ob, nb, rm, gate, up, master, first, second)


def main_kernel(
    tab, hid, wq, og, pre, suf,
    mlp, grad, from_left, from_right,
    h_all, w_all, g_stage, g_all, s_new, s_old, hn, p_acc, part, ho,
    ra2, rb2, rad, rbd, rac, rbc, ca, cb, s_fin,
    c_part, c_sib, c_sum, c_y, c_z,
    send, recv, loc,
):
    dp = lax.axis_index("dp")
    f = lax.axis_index("fsdp")
    z, c = dp // 2, dp % 2
    x, y = f // SIDE, f % SIDE

    def dev(dx=0, dy=0, dz=0, dc=0):
        return (
            (z + dz) % SIDE * 2 + (c + dc) % 2,
            (x + dx) % SIDE * SIDE + (y + dy) % SIDE,
        )

    right = (dp, (f + 1) % POS)
    left = (dp, (f + POS - 1) % POS)
    peers = [dev(dy=d, dc=e) for d in (1, 2, 3) for e in (0, 1)]
    peers += [dev(dx=1), dev(dx=3)]
    peers += [dev(dz=d, dc=e) for d in range(SIDE) for e in (0, 1) if (d, e) != (0, 0)]
    peers += [right, left]

    counter = [0]
    sent = []

    def remote(src, dst, device):
        n = counter[0]
        counter[0] += 1
        copy = pltpu.make_async_remote_copy(
            src_ref=src,
            dst_ref=dst,
            send_sem=send.at[n],
            recv_sem=recv.at[n],
            device_id=device,
            device_id_type=MESH,
        )
        copy.start()
        sent.append(copy)
        return copy

    locals_used = [0]

    def local_copy(src, dst):
        n = locals_used[0]
        locals_used[0] += 1
        copy = pltpu.make_async_copy(src, dst, loc.at[n])
        copy.start()
        return copy

    barrier = pltpu.get_barrier_semaphore()
    for peer in peers:
        pl.semaphore_signal(barrier, inc=1, device_id=peer, device_id_type=MESH)
    pl.semaphore_wait(barrier, len(peers))

    def tok_rows(ref, k, n=1):
        return ref.at[pl.ds(k * TOK, n * TOK)]

    def w_slot(dx, dy):
        pos = (x + dx) % SIDE * SIDE + (y + dy) % SIDE
        return w_all.at[pl.ds(pl.multiple_of(pos * PITCH, PITCH), PITCH)]

    share = pl.multiple_of(dp * 32, 32)
    rel = {d: OFFS.index(d) for d in range(SIDE)}
    g_copies = {}
    for d in (1, 3, 2):
        cols = pl.multiple_of((y + d) % SIDE * COLS, COLS)
        g_copies[d] = remote(
            og.at[pl.ds(share, 32), pl.ds(cols, COLS)], g_stage.at[rel[(-d) % SIDE]], dev(dy=d)
        )
    g_own = local_copy(
        og.at[pl.ds(share, 32), pl.ds(pl.multiple_of(y * COLS, COLS), COLS)], g_stage.at[0]
    )
    w_y = {}
    for d in (1, 3, 2):
        w_y[d] = remote(wq.at[(y + d) % SIDE], w_slot(0, 0), dev(dy=d))
    w_own = local_copy(wq.at[y], w_slot(0, 0))
    wx_plus, wx_minus = {}, {}
    wx_plus[0] = remote(wq.at[y], w_slot(0, 0), dev(dx=1))
    wx_minus[0] = remote(wq.at[y], w_slot(0, 0), dev(dx=3))
    h_plus = remote(hid, tok_rows(h_all, rel[3]), dev(dy=1))
    h_minus = remote(hid, tok_rows(h_all, rel[1]), dev(dy=3))
    h_own = local_copy(hid, tok_rows(h_all, 0))

    for b, (low, wide) in enumerate(NEW_WIN):
        row = lax.broadcasted_iota(jnp.int32, (HALF, 1), 0)
        upper = row >= PITCH
        r = jnp.where(upper, row - PITCH, row)
        start = jnp.where(upper, tab[2, 2 * b + 1], tab[2, 2 * b])
        count = jnp.where(upper, tab[3, 2 * b + 1], tab[3, 2 * b])
        col = jnp.where(r < count, start + r - low, -1)
        lane = lax.broadcasted_iota(jnp.int32, (HALF, wide), 1)
        s_new[pl.ds(HALF * b, HALF), pl.ds(0, wide)] = jnp.where(lane == col, 1.0, 0.0).astype(BF)
    for b, (low, wide) in enumerate(OLD_WIN):
        slot = lax.broadcasted_iota(jnp.int32, (1, 256), 1) + 256 * b
        col = jnp.full((1, 256), -1, jnp.int32)
        for p in range(256 * b // PITCH, min(POS - 1, (256 * b + 255) // PITCH) + 1):
            r = slot - p * PITCH
            col = jnp.where((r >= 0) & (r < tab[1, p]), tab[0, p] + r - low, col)
        row = lax.broadcasted_iota(jnp.int32, (wide, 256), 0)
        s_old[pl.ds(0, wide), pl.ds(256 * b, 256)] = jnp.where(row == col, 1.0, 0.0).astype(BF)

    g_own.wait()
    for d in (1, 3, 2):
        g_copies[d].wait_recv()

    def g_slot(k):
        return g_all.at[pl.ds(k * TOK + share, 32)]

    g_out = []
    for e, d in ((1, 0), (0, 1), (0, 3), (1, 1), (1, 3), (0, 2), (1, 2)):
        g_out.append([remote(g_stage.at[k], g_slot(k), dev(dz=d, dc=e)) for k in range(SIDE)])
    g_loc = [local_copy(g_stage.at[k], g_slot(k)) for k in range(SIDE)]

    for d in (1, 3, 2):
        w_y[d].wait_recv()
        piece = w_slot(0, -d)
        wx_plus[d] = remote(piece, piece, dev(dx=1))
        wx_minus[d] = remote(piece, piece, dev(dx=3))
    w_far = []
    for d in (0, 1, 3, 2):
        wx_plus[d].wait_recv()
        wx_minus[d].wait_recv()
        if d in (0, 1):
            piece = w_slot(-1, -d)
            w_far.append(remote(piece, piece, dev(dx=1)))
        else:
            piece = w_slot(1, -d)
            w_far.append(remote(piece, piece, dev(dx=3)))

    h_plus.wait_recv()
    h_minus.wait_recv()
    h_far_plus = remote(
        h_all.at[pl.ds(rel[3] * TOK, 128)], h_all.at[pl.ds(rel[2] * TOK, 128)], dev(dy=1)
    )
    h_far_minus = remote(
        h_all.at[pl.ds(rel[1] * TOK + 128, 128)],
        h_all.at[pl.ds(rel[2] * TOK + 128, 128)],
        dev(dy=3),
    )
    m_right = remote(suf, from_left, right)
    m_left = remote(pre, from_right, left)

    h_own.wait()
    for k in range(SIDE):
        g_loc[k].wait()
    for group in g_out:
        for copy in group:
            copy.wait_recv()

    def grad_rows(b, first, count):
        low, wide = NEW_WIN[b]
        toks = pl.ds(first * TOK, count * TOK)
        rows = pl.ds(HALF * b, HALF)
        hn[:, pl.ds(0, count * TOK)] = lax.dot_general(
            s_new[rows, pl.ds(0, wide)],
            h_all[toks, pl.ds(low, wide)],
            (((1,), (1,)), ((), ())),
            preferred_element_type=F32,
        ).astype(BF)
        return jnp.dot(
            hn[:, pl.ds(0, count * TOK)], g_all[toks, :], preferred_element_type=F32
        )

    for b in range(8):
        p_acc[b] = grad_rows(b, 0, 3)
    h_far_plus.wait_recv()
    h_far_minus.wait_recv()
    for b in range(8):
        part[b] = (p_acc[b] + grad_rows(b, 3, 1)).astype(BF)

    def slab(dx, half):
        return part.at[(x + dx) % SIDE * 2 + half]

    copy_b2 = remote(slab(2, 1), rb2, dev(dx=1))
    copy_a2 = remote(slab(2, 0), ra2, dev(dx=3))
    copy_ad = remote(slab(1, 0), rad, dev(dx=1))
    copy_bd = remote(slab(3, 1), rbd, dev(dx=3))

    w_own.wait()
    for copy in w_far:
        copy.wait_recv()

    def forward(k):
        toks = pl.ds(pl.multiple_of(k * TOK, TOK), TOK)
        for b, (low, wide) in enumerate(OLD_WIN):
            ho[:, pl.ds(256 * b, 256)] = jnp.dot(
                h_all[toks, pl.ds(low, wide)],
                s_old[pl.ds(0, wide), pl.ds(256 * b, 256)],
                preferred_element_type=F32,
            ).astype(BF)
        c_part[k] = jnp.dot(ho[...], w_all[...], preferred_element_type=F32).astype(BF)

    @pl.loop(0, SIDE)
    def _(k):
        forward(k)

    theirs = pl.multiple_of((1 - c) * 128, 128)
    mine = pl.multiple_of(c * 128, 128)
    copy_sib = remote(c_part.at[:, pl.ds(theirs, 128)], c_sib, dev(dc=1))

    copy_b2.wait_recv()
    cb[...] = (rb2[...].astype(F32) + part[(x + 1) % SIDE * 2 + 1].astype(F32)).astype(BF)
    copy_bc = remote(cb, rbc, dev(dx=1))
    copy_a2.wait_recv()
    ca[...] = (ra2[...].astype(F32) + part[(x + 3) % SIDE * 2].astype(F32)).astype(BF)
    copy_ac = remote(ca, rac, dev(dx=3))

    copy_sib.wait_recv()
    c_sum[...] = (
        c_part[:, pl.ds(mine, 128), :].astype(F32) + c_sib[...].astype(F32)
    ).astype(BF)
    c_copies = []
    for d in (2, 1, 3, 0):
        for e in (0, 1):
            src = c_sum.at[rel[d], :, pl.ds(pl.multiple_of((c + e) % 2 * 512, 512), 512)]
            dst = c_y.at[y, pl.ds(mine, 128)]
            if (d, e) == (0, 0):
                c_own = local_copy(src, dst)
            else:
                c_copies.append(remote(src, dst, dev(dy=d, dc=e)))
    c_own.wait()
    for copy in c_copies:
        copy.wait_recv()
    z_copies = [remote(c_y.at[(z + d) % SIDE], c_z.at[d - 1], dev(dz=d)) for d in (2, 1, 3)]

    copy_ad.wait_recv()
    copy_ac.wait_recv()
    total = part[x * 2].astype(F32) + rad[...].astype(F32) + rac[...].astype(F32)
    s_fin[pl.ds(0, 2)] = total.astype(BF).reshape(2, PITCH, COLS)
    copy_bd.wait_recv()
    copy_bc.wait_recv()
    total = part[x * 2 + 1].astype(F32) + rbd[...].astype(F32) + rbc[...].astype(F32)
    s_fin[pl.ds(2, 2)] = total.astype(BF).reshape(2, PITCH, COLS)
    r_copies = [remote(s_fin.at[(y + d) % SIDE], grad.at[y], dev(dy=d)) for d in (2, 1, 3)]
    r_own = local_copy(s_fin.at[y], grad.at[y])

    for copy in z_copies:
        copy.wait_recv()
    mlp[...] = (
        c_y[z].astype(F32) + c_z[0].astype(F32) + c_z[1].astype(F32) + c_z[2].astype(F32)
    )
    r_own.wait()
    for copy in r_copies:
        copy.wait_recv()
    m_right.wait_recv()
    m_left.wait_recv()
    for copy in sent:
        copy.wait_send()


def exchange(tab, hid, wq, og, pre, suf):
    anywhere = pl.BlockSpec(memory_space=pl.ANY)
    vmem = pl.BlockSpec(memory_space=pltpu.VMEM)
    half = pltpu.VMEM((HALF, COLS), BF)
    return pl.pallas_call(
        main_kernel,
        in_specs=[pl.BlockSpec(memory_space=pltpu.SMEM)] + [anywhere] * 5,
        out_specs=[vmem, anywhere, anywhere, anywhere],
        out_shape=[
            jax.ShapeDtypeStruct((TOK, 512), F32),
            jax.ShapeDtypeStruct((SIDE, PITCH, COLS), BF),
            jax.ShapeDtypeStruct((3, EDGE, D), BF),
            jax.ShapeDtypeStruct((3, EDGE, D), BF),
        ],
        scratch_shapes=[
            pltpu.VMEM((SIDE * TOK, HIDP), BF),
            pltpu.VMEM((SLOTS, COLS), BF),
            pltpu.VMEM((SIDE, 32, COLS), BF),
            pltpu.VMEM((SIDE * TOK, COLS), BF),
            pltpu.VMEM((SLOTS, NEW_MAX), BF),
            pltpu.VMEM((OLD_MAX, SLOTS), BF),
            pltpu.VMEM((HALF, SIDE * TOK), BF),
            pltpu.VMEM((8, HALF, COLS), F32),
            pltpu.VMEM((8, HALF, COLS), BF),
            pltpu.VMEM((TOK, SLOTS), BF),
            half, half, half, half, half, half, half, half,
            pltpu.VMEM((SIDE, PITCH, COLS), BF),
            pltpu.VMEM((SIDE, TOK, COLS), BF),
            pltpu.VMEM((SIDE, 128, COLS), BF),
            pltpu.VMEM((SIDE, 128, COLS), BF),
            pltpu.VMEM((SIDE, TOK, 512), BF),
            pltpu.VMEM((3, TOK, 512), BF),
            pltpu.SemaphoreType.DMA((80,)),
            pltpu.SemaphoreType.DMA((80,)),
            pltpu.SemaphoreType.DMA((10,)),
        ],
        compiler_params=pltpu.CompilerParams(
            collective_id=0, has_side_effects=True, vmem_limit_bytes=63 * 1024 * 1024
        ),
        name="exchange",
    )(tab, hid, wq, og, pre, suf)


def adam_kernel(scale, tab, master, first, second, left, right, grad, o_m, o_1, o_2, buf):
    me = lax.axis_index("fsdp")
    old_count = tab[1, me]
    count = tab[3, me]
    shift = jnp.clip(tab[2, me] - tab[0, me], -EDGE, CAP + EDGE)
    row = lax.broadcasted_iota(jnp.int32, (CAP, 128), 0)
    live = row < count
    for j in range(master.shape[2] // 128):
        lanes = pl.ds(128 * j, 128)
        moved = []
        for a, ref in enumerate((master, first, second)):
            own = buf.at[3 * j + a]
            own[pl.ds(0, EDGE), :] = left[a, :, lanes].astype(F32)
            own[pl.ds(EDGE, CAP), :] = ref[0, :, lanes]
            own[pl.ds(EDGE + old_count, EDGE), :] = right[a, :, lanes].astype(F32)
            moved.append(own[pl.ds(EDGE + shift, CAP), :])
        weight, one, two = moved
        g = grad[0, pl.ds(0, CAP), lanes].astype(F32) * scale
        one = 0.9 * one + 0.1 * g
        two = 0.95 * two + 0.05 * g * g
        weight = weight - 0.001 * (one / (jnp.sqrt(two) + 1e-08) + 0.1 * weight)
        o_m[0, :, lanes] = jnp.where(live, weight, 0.0)
        o_1[0, :, lanes] = jnp.where(live, one, 0.0)
        o_2[0, :, lanes] = jnp.where(live, two, 0.0)


def adam(tab, master, first, second, left, right, grad, scale):
    wide = 512
    per = COLS // wide
    state = pl.BlockSpec((1, CAP, wide), lambda i: (0, 0, i))
    edge = pl.BlockSpec((3, EDGE, wide), lambda i: (0, 0, i))
    return pl.pallas_call(
        functools.partial(adam_kernel, scale),
        grid=(D // wide,),
        in_specs=[
            pl.BlockSpec(memory_space=pltpu.SMEM),
            state, state, state, edge, edge,
            pl.BlockSpec((1, PITCH, wide), lambda i: (i // per, 0, i % per)),
        ],
        out_specs=[state, state, state],
        out_shape=[jax.ShapeDtypeStruct((1, CAP, D), F32)] * 3,
        scratch_shapes=[pltpu.VMEM((3 * wide // 128, 400, 128), F32)],
        name="adam",
    )(tab, master, first, second, left, right, grad)


def local(gate_act, up_act, out_grad, master_old, moment1_old, moment2_old, old_bounds, new_bounds, rank_map):
    scale = 1.0 / math.sqrt(gate_act.shape[0] * lax.axis_size("fsdp"))
    tab, hid, wq, pre, suf = prep(
        old_bounds, new_bounds, rank_map, gate_act, up_act, master_old, moment1_old, moment2_old
    )
    mlp, grad, left, right = exchange(tab, hid, wq, out_grad, pre, suf)
    master, first, second = adam(
        tab, master_old, moment1_old, moment2_old, left, right, grad, scale
    )
    return mlp, master, first, second


def solution(mesh):
    act = P("fsdp", "dp")
    state = P("dp", "fsdp", None)
    table = P("dp", None)
    return jax.shard_map(
        local,
        mesh=mesh,
        in_specs=(act, act, P("fsdp", None), state, state, state, table, table, table),
        out_specs=(act, state, state, state),
        check_vma=False,
    )
```

time: 451 us -> 172 us (0.38)
  Pallas kernels: 0 us -> 166 us
  waiting for transfers between devices: 150 us -> 0 us
  matrix products: 95.4 us -> 0 us
  other arithmetic: 83.4 us -> 0 us
  local copies, waits for them, and re-layouts: 66.4 us -> 4.51 us
  loops' own time: 31.3 us -> 0 us
  between operations: 17.8 us -> 0.66 us
  starting transfers between devices: 6.23 us -> 0 us
    pallas_call x0 -> x3, Pallas kernels: none -> 166 us  [the longest x1 149 us: exchange(): pl.pallas_call(main_kernel, in_specs=[pl.BlockSpec(memory_space=pltpu.SME...]
    all_gather x1 -> x0, waiting for transfers between devices: 98.5 us -> none  [block_product(): piece = lax.all_gather(weight_shard, 'fsdp', axis=0, tiled=True)]
    dot_general x17 -> x0, matrix products: 95.4 us -> none  [the longest x16 85.1 us: one_shard(): return carry + jnp.dot(columns, block, preferred_element_type=jnp.float32)]
    another operation x1 -> x0, loops' own time: 31.3 us -> none  [block_product(): return lax.fori_loop(0, shard_count, one_shard, empty)]
    ppermute x2 -> x0, waiting for transfers between devices: 29.8 us -> none  [passed_along(): lax.ppermute(value, axis, [(source, source + steps) for source in range(l...]
    gather x2 -> x0, local copies, waits for them, and re-layouts: 24.9 us -> none  [the longest x1 17.2 us: migrate(): chosen = jnp.take(source, index, axis=1)]
    concatenate x2 -> x0, local copies, waits for them, and re-layouts: 23.2 us -> none  [the longest x1 23.1 us: migrate(): source = jnp.concatenate([from_left, stacked, from_right], axis=1)]
    reduce_scatter x1 -> x0, waiting for transfers between devices: 21.3 us -> none  [local(): lax.psum_scatter(block_part.astype(jnp.bfloat16), 'dp', scatter_dimension...]
  transfers between devices with their start and end apart: 5 -> 0, of which waited for: 4 -> 0; matrix products, arithmetic and copies ran while one was open for 33% -> 0% of each run, Pallas kernels for 0% -> 0%
where the time goes in v1:
time: 172 us; the launch traced here: 171 us
  Pallas kernels  166 us (97%)
  local copies, waits for them, and re-layouts  4.51 us (3%)
    pallas_call x1, Pallas kernels, exchange(): pl.pallas_call(main_kernel, in_specs=[pl.BlockSpec(memory_space=pltpu.SME...  149 us
    pallas_call x1, Pallas kernels, adam(): pl.pallas_call(functools.partial(adam_kernel, scale), grid=(D // wide,),...  10.2 us
    pallas_call x1, Pallas kernels, prep(): pl.pallas_call(prep_kernel, grid=(4,), in_specs=[smem, smem, smem, act, a...  6.46 us
    unnamed x7, local copies, waits for them, and re-layouts  4.51 us

profile of v1, /device:TPU:0, one launch (start us, length us, event | category | flops | bytes accessed | tf_op | source)
XLA Modules:
  0.0 170.8 jit_solution(10770301526364294946)
XLA Ops:
  0.6 0.0 copy-start
  0.6 2.3 %copy.13.gate = bf16[256,1856]{1,0:T(8,128)(2,1)} copy(bf16[256,1856]{0,1:T(8,128)(2,1)} %param.9) | data formatting | bytes 1900544 | tf_op args[0]
  3.0 0.0 copy-done
  3.0 1.4 copy.14.up
  4.4 6.5 %prep.1 = (s32[4,16]{1,0:T(4,128)}, bf16[256,1920]{1,0:T(8,128)(2,1)}, bf16[4,144,1024]{2,1,0:T(8,128)(2,1)}, bf16[3,64,4096]{2,1,0:T(8,128)(2,1)}, bf16[3,64,4096]{2,1,0:T(8,128)(2,1)}) custom-call(s32[1,17]{1,0:T(1,128)} %ob.1, s32[1,16]{1,0:T(1,128)} %nb.1, s32[1,16]{1,0:T(1,128)} %rm.1, bf16[256,1856]{1,0:T(8,128)(2,1)} %copy.13.gate, ...), custom_call_target="tpu_custom_call" | custom-call | tf_op jit(solution)/shard_map/prep/pallas_call | solution.py:87
  10.8 149.0 %exchange.1 = (f32[256,512]{1,0:T(8,128)}, bf16[4,144,1024]{2,1,0:T(8,128)(2,1)}, bf16[3,64,4096]{2,1,0:T(8,128)(2,1)}, bf16[3,64,4096]{2,1,0:T(8,128)(2,1)}) custom-call(s32[4,16]{1,0:T(4,128)} %get-tuple-element.16.tab, bf16[256,1920]{1,0:T(8,128)(2,1)} %get-tuple-element.17.hid, bf16[4,144,1024]{2,1,0:T(8,128)(2,1)} %get-tuple-element.18.wq, ...), custom_call_target="tpu_custom_call" | custom-call | tf_op jit(solution)/shard_map/exchange/pallas_call | solution.py:368
  159.8 0.0 copy-start.1
  159.8 10.2 %adam.1 = (f32[1,136,4096]{2,1,0:T(8,128)}, f32[1,136,4096]{2,1,0:T(8,128)}, f32[1,136,4096]{2,1,0:T(8,128)}) custom-call(s32[4,16]{1,0:T(4,128)} %get-tuple-element.16.tab, f32[1,136,4096]{2,1,0:T(8,128)} %master.3, f32[1,136,4096]{2,1,0:T(8,128)} %first.3, f32[1,136,4096]{2,1,0:T(8,128)} %second.3, bf16[3,64,4096]{2,1,0:T(8,128)(2,1)} %get-tuple-element.22.left, ...), custom_call_target="tpu_custom_call" | custom-call | tf_op jit(solution)/shard_map/adam/pallas_call | solution.py:438
  170.0 0.0 copy-done.1
  170.0 0.8 copy.16
Async XLA Ops:
  0.6 2.3 %copy-start = (bf16[256,1856]{0,1:T(8,128)(2,1)S(1)}, bf16[256,1856]{0,1:T(8,128)(2,1)}, u32[]{:S(2)}) copy-start(bf16[256,1856]{0,1:T(8,128)(2,1)} %param.10) | copy-start | bytes 2850820
  159.8 10.2 %copy-start.1 = (f32[256,512]{1,0:T(8,128)S(1)}, f32[256,512]{1,0:T(8,128)}, u32[]{:S(2)}) copy-start(f32[256,512]{1,0:T(8,128)} %get-tuple-element.32) | copy-start | bytes 1572868
